TPU v7x, 128 devices: a whole 4x4x4 slice. The times are simulated.
128 devices in a mesh: blk: 64 (over z, y, x_hi, core), rows: 2 (over x_lo).
Axes of the slice: x: 4 (x_hi: 2, x_lo: 2; x = x_hi * 2 + x_lo), y: 4, z: 4, core: 2. Of those that a mesh axis runs over, the one named last changes fastest.
Arguments:
- panel: bfloat16 [4, 512, 393216], P(None, 'rows', 'blk'), may hold values from -0.009765625 to 0.009765625
- solved: bfloat16 [393216, 1024], P('blk'), may hold values from -6 to 6
- loads: float32 [4, 512, 1024], P(None, 'rows'), may hold values from -6 to 6
- window: bfloat16 [4, 512, 2048], P(None, 'rows'), may hold values from -0.25 to 0.25
- inverses: bfloat16 [4, 512, 512], P(None, 'rows'), as said below
Outputs:
- unknowns: bfloat16 [4, 512, 1024], P(None, 'rows')
Inputs may be any that keep to these rules, and one draw needn't show every extreme that they name: inverses[i] is lower triangular, the inverse of the factor's i-th diagonal block.
All inputs are finite; a program needn't handle non-finite values.
Results may differ from a plain program's by a relative error of at most 0.01.
Values may be sent and summed in bfloat16 or wider, within the bound.
A program may use at most 128 MiB of HBM per device.

v0:
```python
import jax
import jax.numpy as jnp
from jax import lax
from jax.sharding import PartitionSpec as P


def shards(panel, solved, loads, window, inverses):
    partial_value = jnp.einsum("ksc,cr->ksr", panel, solved, preferred_element_type=jnp.float32)
    totals = lax.psum(partial_value, "blk")
    remaining = loads - totals
    block_size = inverses.shape[2]
    step_count = loads.shape[0]
    full_blocks = []
    own_rows = []
    for current in range(step_count):
        residual = remaining[current]
        for earlier in range(current):
            coupling = window[current][:, earlier * block_size : (earlier + 1) * block_size]
            residual = residual - jnp.dot(
                coupling, full_blocks[earlier], preferred_element_type=jnp.float32
            )
        residual = residual.astype(jnp.bfloat16)
        inverse_now = inverses[current]
        solved_part = jnp.dot(
            inverse_now,
            lax.all_gather(residual, "rows", axis=0, tiled=True),
            preferred_element_type=jnp.float32,
        ).astype(jnp.bfloat16)
        own_rows.append(solved_part)
        if current + 1 < step_count:
            full_blocks.append(lax.all_gather(solved_part, "rows", axis=0, tiled=True))
    result = jnp.stack(own_rows)
    return result


def solution(mesh):
    placed = (
        P(None, "rows", "blk"),
        P("blk", None),
        P(None, "rows", None),
        P(None, "rows", None),
        P(None, "rows", None),
    )
    return jax.shard_map(
        shards, mesh=mesh, in_specs=placed, out_specs=P(None, "rows", None), check_vma=False
    )
```

profile of v0, /device:TPU:1, one launch (start us, length us, event | category | flops | bytes accessed | tf_op | source)
XLA Modules:
  0.0 892.1 jit_solution(10524054517992434693)
XLA Ops:
  6.5 0.0 all-reduce.2.cloned.1.call-start
  6.5 19.0 %fusion = f32[4,256,1024]{2,1,0:T(8,128)} fusion(bf16[4,256,6144]{2,1,0:T(8,128)(2,1)} %param.5, bf16[6144,1024]{1,0:T(8,128)(2,1)} %param.6), kind=kOutput, calls=%fused_computation | convolution fusion | flops 12884901888 | bytes 29360128 | tf_op jit(solution)/shard_map/ksc,cr->ksr/dot_general | solution.py:8
  25.6 0.0 all-reduce.2.cloned.1.call-update
  25.6 0.0 all-gather.21.cloned.1.call-start
  25.7 653.3 %all-reduce.2.cloned.1.call-done = f32[4,256,1024]{2,1,0:T(8,128)} async-done(((f32[4,256,1024]{2,1,0:T(8,128)}), f32[4,256,1024]{2,1,0:T(8,128)}) %all-reduce.2.cloned.1.call-update) | async-done | bytes 4194320 | tf_op jit(solution)/shard_map/psum | solution.py:9
  679.0 4.4 sub.21
  683.4 0.0 copy-start
  683.4 1.9 copy-done
  685.3 0.9 slice.123
  686.2 0.0 all-gather.21.cloned.1.call-update
  686.2 0.0 all-gather.9.cloned.1.call-start
  686.3 24.5 %all-gather.21.cloned.1.call-done = bf16[1,512,1024]{2,1,0:T(8,128)(2,1)} async-done(((bf16[1,256,1024]{2,1,0:T(8,128)(2,1)}), bf16[1,512,1024]{2,1,0:T(8,128)(2,1)}) %all-gather.21.cloned.1.call-update) | async-done | bytes 1048592 | tf_op jit(solution)/shard_map/all_gather | solution.py:26
  710.7 2.6 convolution_convert_fusion.3
  713.3 0.0 all-gather.9.cloned.1.call-update
  713.3 0.0 all-gather.11.cloned.1.call-start
  713.4 3.1 slice_bitcast_fusion.3
  716.5 21.7 %all-gather.9.cloned.1.call-done = bf16[512,1024]{0,1:T(8,128)(2,1)} async-done(((bf16[256,1024]{0,1:T(8,128)(2,1)}), bf16[512,1024]{0,1:T(8,128)(2,1)}) %all-gather.9.cloned.1.call-update) | async-done | bytes 1048592 | tf_op jit(solution)/shard_map/all_gather | solution.py:31
  738.2 0.0 copy-start.1
  738.2 2.9 fusion.10
  741.1 0.0 all-gather.11.cloned.1.call-update
  741.1 0.0 all-gather.13.cloned.1.call-start
  741.2 24.9 %all-gather.11.cloned.1.call-done = bf16[512,1024]{1,0:T(8,128)(2,1)} async-done(((bf16[256,1024]{1,0:T(8,128)(2,1)}), bf16[512,1024]{1,0:T(8,128)(2,1)}) %all-gather.11.cloned.1.call-update) | async-done | bytes 1048592 | tf_op jit(solution)/shard_map/all_gather | solution.py:26
  766.1 2.6 convolution_convert_fusion.2
  768.6 0.0 all-gather.13.cloned.1.call-update
  768.6 0.0 all-gather.15.cloned.1.call-start
  768.7 24.8 %all-gather.13.cloned.1.call-done = bf16[512,1024]{0,1:T(8,128)(2,1)} async-done(((bf16[256,1024]{0,1:T(8,128)(2,1)}), bf16[512,1024]{0,1:T(8,128)(2,1)}) %all-gather.13.cloned.1.call-update) | async-done | bytes 1048592 | tf_op jit(solution)/shard_map/all_gather | solution.py:31
  793.5 0.0 copy-start.2
  793.5 1.8 convolution_bitcast_fusion.3
  795.3 0.0 copy-done.1
  795.3 2.5 fusion.9
  797.8 0.0 all-gather.15.cloned.1.call-update
  797.8 0.0 all-gather.17.cloned.1.call-start
  797.9 24.9 %all-gather.15.cloned.1.call-done = bf16[512,1024]{1,0:T(8,128)(2,1)} async-done(((bf16[256,1024]{1,0:T(8,128)(2,1)}), bf16[512,1024]{1,0:T(8,128)(2,1)}) %all-gather.15.cloned.1.call-update) | async-done | bytes 1048592 | tf_op jit(solution)/shard_map/all_gather | solution.py:26
  822.7 2.5 convolution_convert_fusion.1
  825.3 0.0 all-gather.17.cloned.1.call-update
  825.3 0.0 all-gather.19.cloned.1.call-start
  825.4 0.0 copy-done.2
  825.4 1.4 convolution_bitcast_fusion.1
  826.8 23.4 %all-gather.17.cloned.1.call-done = bf16[512,1024]{0,1:T(8,128)(2,1)} async-done(((bf16[256,1024]{0,1:T(8,128)(2,1)}), bf16[512,1024]{0,1:T(8,128)(2,1)}) %all-gather.17.cloned.1.call-update) | async-done | bytes 1048592 | tf_op jit(solution)/shard_map/all_gather | solution.py:31
  850.2 1.7 convolution_bitcast_fusion
  851.9 2.6 fusion.8
  854.5 0.0 all-gather.19.cloned.1.call-update
  854.5 24.9 %all-gather.19.cloned.1.call-done = bf16[512,1024]{1,0:T(8,128)(2,1)} async-done(((bf16[256,1024]{1,0:T(8,128)(2,1)}), bf16[512,1024]{1,0:T(8,128)(2,1)}) %all-gather.19.cloned.1.call-update) | async-done | bytes 1048592 | tf_op jit(solution)/shard_map/all_gather | solution.py:26
  879.5 1.7 fusion.11
  881.2 1.6 pad_maximum_fusion
  882.8 2.4 copy.6
Async XLA Ops:
  6.5 672.4 %all-reduce.2.cloned.1.call-start = ((), (), s32[]{:S(2)}) async-start(), calls=%async_computation | async-start | bytes 8388608 | tf_op jit(solution)/shard_map/psum | solution.py:9
  25.6 685.1 %all-gather.21.cloned.1.call-start = ((), (), s32[]{:S(2)}) async-start(), calls=%async_computation.7 | async-start | bytes 1572864 | tf_op jit(solution)/shard_map/all_gather | solution.py:26
  683.4 1.9 copy-start
  686.2 52.0 %all-gather.9.cloned.1.call-start = ((), (), s32[]{:S(2)}) async-start(), calls=%async_computation.1 | async-start | bytes 1572864 | tf_op jit(solution)/shard_map/all_gather | solution.py:31
  713.3 52.7 %all-gather.11.cloned.1.call-start = ((), (), s32[]{:S(2)}) async-start(), calls=%async_computation.2 | async-start | bytes 1572864 | tf_op jit(solution)/shard_map/all_gather | solution.py:26
  738.2 57.1 %copy-start.1 = (bf16[512,1024]{0,1:T(8,128)(2,1)S(1)}, bf16[512,1024]{0,1:T(8,128)(2,1)}, u32[]{:S(2)}) copy-start(bf16[512,1024]{0,1:T(8,128)(2,1)} %all-gather.9.cloned.1.call-done) | copy-start | bytes 3145732
  741.1 52.4 %all-gather.13.cloned.1.call-start = ((), (), s32[]{:S(2)}) async-start(), calls=%async_computation.3 | async-start | bytes 1572864 | tf_op jit(solution)/shard_map/all_gather | solution.py:31
  768.6 54.1 %all-gather.15.cloned.1.call-start = ((), (), s32[]{:S(2)}) async-start(), calls=%async_computation.4 | async-start | bytes 1572864 | tf_op jit(solution)/shard_map/all_gather | solution.py:26
  793.5 31.8 %copy-start.2 = (bf16[512,1024]{0,1:T(8,128)(2,1)S(1)}, bf16[512,1024]{0,1:T(8,128)(2,1)}, u32[]{:S(2)}) copy-start(bf16[512,1024]{0,1:T(8,128)(2,1)} %all-gather.13.cloned.1.call-done) | copy-start | bytes 3145732
  797.8 52.4 %all-gather.17.cloned.1.call-start = ((), (), s32[]{:S(2)}) async-start(), calls=%async_computation.5 | async-start | bytes 1572864 | tf_op jit(solution)/shard_map/all_gather | solution.py:31
  825.3 54.2 %all-gather.19.cloned.1.call-start = ((), (), s32[]{:S(2)}) async-start(), calls=%async_computation.6 | async-start | bytes 1572864 | tf_op jit(solution)/shard_map/all_gather | solution.py:26
Sparse Core Ops, SparseCore 0:
  25.7 653.1 all-reduce.1
  686.3 24.3 all-gather.20
  713.4 24.7 all-gather.8
  741.3 24.7 all-gather.10
  768.8 24.7 all-gather.12
  797.9 24.7 all-gather.14
  825.4 24.7 all-gather.16
  854.7 24.7 all-gather.18
where the time goes:
time: 892 us
  waiting for transfers between devices  823 us (92%)
  matrix products  41.4 us (5%)
  between operations  13.6 us (2%)
    psum x1, waiting for transfers between devices, shards(): totals = lax.psum(partial_value, 'blk')  653 us
    all_gather x4, waiting for transfers between devices, shards(): lax.all_gather(residual, 'rows', axis=0, tiled=True)  99.1 us
    all_gather x3, waiting for transfers between devices, shards(): full_blocks.append(lax.all_gather(solved_part, 'rows', axis=0, tiled=True))  69.9 us
    dot_general x1, matrix products, shards(): jnp.einsum('ksc,cr->ksr', panel, solved, preferred_element_type=jnp.float32)  19 us
  transfers between devices with their start and end apart: 8, of which 8 were waited for; matrix products, arithmetic and copies ran while one was open for 1% of the time, Pallas kernels for 0%

commit v1 on v0

v1 whole, which is shorter than its diff:
```python
import jax
import jax.numpy as jnp
from jax import lax
from jax.experimental import pallas as pl
from jax.experimental.pallas import tpu as pltpu
from jax.sharding import PartitionSpec as P

F32 = jnp.float32
BF16 = jnp.bfloat16
LANES = 128
KPARTS = 4


def kernel(
    panel_ref, solved_ref, loads_ref, window_ref, inv_ref, out_ref,
    pv, sv, acc, core_out, core_in, a_out, a_in, b_buf, x_buf, loads_v,
    w1, w2, w3, inv_v, u_all, coupled, own_u,
    local_sem, w_send, w_recv, f_send, f_recv, c_send, c_recv,
    a_send, a_recv, b_send, b_recv, x_send, x_recv, g_send, g_recv, p_send, p_recv,
):
    steps, half, depth = pv.shape
    block = 2 * half
    width = sv.shape[2]
    kpart = depth // KPARTS

    blk = lax.axis_index("blk")
    xl = lax.axis_index("rows")
    core = blk % 2
    xh = (blk // 2) % 2
    y = (blk // 4) % 4
    z = blk // 16
    x = xh * 2 + xl
    a = z * (1 - core) + y * core
    b = y * (1 - core) + z * core
    other = 1 - core

    def device(z_, y_, xh_, xl_, core_):
        return {"blk": ((z_ * 4 + y_) * 2 + xh_) * 2 + core_, "rows": xl_}

    partner = device(z, y, xh, xl, other)

    def a_peer(d):
        n = (a + d) % 4
        return device(n * (1 - core) + b * core, b * (1 - core) + n * core, xh, xl, core)

    def b_peer(d):
        n = (b + d) % 4
        return device(a * (1 - core) + n * core, n * (1 - core) + a * core, xh, xl, core)

    def x_peer(d):
        n = (x + d) % 4
        return device(z, y, n // 2, n % 2, core)

    side = [device(z, y, xh, 1 - xl, core), device(z, y, 1 - xh, 1 - xl, core)]

    def remote(src, dst, send, recv, target):
        return pltpu.make_async_remote_copy(
            src_ref=src, dst_ref=dst, send_sem=send, recv_sem=recv,
            device_id=target, device_id_type=pl.DeviceIdType.MESH,
        )

    started = []

    def go(copy):
        copy.start()
        started.append(copy)

    def cols(core_, a_):
        return pl.ds(pl.multiple_of(core_ * width + a_ * LANES, LANES), LANES)

    head = []
    for k in range(KPARTS):
        ks = pl.ds(k * kpart, kpart)
        head.append((
            pltpu.make_async_copy(panel_ref.at[0, :, ks], pv.at[0, :, ks], local_sem.at[2 * k]),
            pltpu.make_async_copy(
                solved_ref.at[ks, pl.ds(pl.multiple_of(other * width, width), width)],
                sv.at[0, ks, :], local_sem.at[2 * k + 1]),
        ))
    base = 2 * KPARTS
    own_half = pltpu.make_async_copy(
        solved_ref.at[:, pl.ds(pl.multiple_of(core * width, width), width)],
        sv.at[1], local_sem.at[base])
    panels = [None] + [
        pltpu.make_async_copy(panel_ref.at[i], pv.at[i], local_sem.at[base + i])
        for i in range(1, steps)
    ]
    windows = [None, w1, w2, w3]
    small = [
        pltpu.make_async_copy(loads_ref.at[:, :, cols(core, a)], loads_v, local_sem.at[base + 4]),
        pltpu.make_async_copy(inv_ref, inv_v.at[:, xl], local_sem.at[base + 5]),
    ] + [
        pltpu.make_async_copy(
            window_ref.at[i, :, pl.ds(0, i * block)], windows[i].at[xl], local_sem.at[base + 5 + i])
        for i in range(1, steps)
    ]

    for pair in head[:3]:
        for copy in pair:
            copy.start()

    barrier = pltpu.get_barrier_semaphore()
    greeted = [partner]
    for d in (1, 2, 3):
        greeted += [a_peer(d), b_peer(d), x_peer(d)]
    for peer in greeted:
        pl.semaphore_signal(barrier, inc=1, device_id=peer, device_id_type=pl.DeviceIdType.MESH)

    quarter = half // 4

    def share(d, core_):
        return pl.ds(pl.multiple_of((d * 2 + core_) * quarter, quarter), quarter)

    def factor_views(rows_half, rows):
        return [inv_v.at[pl.ds(0, steps - 1), rows_half, rows, :]] + [
            windows[i].at[rows_half, rows, :] for i in range(1, steps)
        ]

    def factor_send(d):
        rows = share(d, core)
        sources = [inv_ref.at[pl.ds(0, steps - 1), rows, :]] + [
            window_ref.at[i, rows, pl.ds(0, i * block)] for i in range(1, steps)
        ]
        return [
            remote(s, t, w_send.at[d, j], w_recv.at[d, j], side[d])
            for j, (s, t) in enumerate(zip(sources, factor_views(xl, rows)))
        ]

    def factor_arrive(d):
        views = factor_views(1 - xl, share(d, core))
        return [remote(v, v, w_send.at[d, j], w_recv.at[d, j], side[d]) for j, v in enumerate(views)]

    def factor_forward(d):
        views = factor_views(1 - xl, share(d, core))
        return [remote(v, v, f_send.at[d, j], f_recv.at[d, j], partner) for j, v in enumerate(views)]

    def factor_forwarded(d):
        views = factor_views(1 - xl, share(d, other))
        return [remote(v, v, f_send.at[d, j], f_recv.at[d, j], partner) for j, v in enumerate(views)]

    def forward_factor(parts):
        for j in parts:
            for d in (0, 1):
                factor_arrive(d)[j].wait_recv()
                go(factor_forward(d)[j])

    def core_copy(i):
        return remote(core_out.at[i], core_in.at[i], c_send.at[i], c_recv.at[i], partner)

    def send_core(i):
        core_out[i] = acc[...].astype(BF16)
        go(core_copy(i))

    def a_copy(i, d):
        return remote(a_out.at[i, (a + d) % 4], a_in.at[i, d - 1],
                      a_send.at[i, d - 1], a_recv.at[i, d - 1], a_peer(d))

    def send_a(i):
        core_copy(i).wait_recv()
        for n in range(4):
            at = slice(n * LANES, (n + 1) * LANES)
            a_out[i, n] = (acc[:, at] + core_in[i, :, at].astype(F32)).astype(BF16)
        for d in (2, 1, 3):
            go(a_copy(i, d))

    def b_copy(i, d):
        return remote(b_buf.at[i, b], b_buf.at[i, b], b_send.at[i, d - 1], b_recv.at[i, d - 1], b_peer(d))

    def send_b(i):
        total = a_out[i, a].astype(F32)
        for d in (1, 3, 2):
            a_copy(i, d).wait_recv()
            total = total + a_in[i, d - 1].astype(F32)
        b_buf[i, b] = total.astype(BF16)
        for d in (2, 1, 3):
            go(b_copy(i, d))

    def x_copy(i, d):
        return remote(x_buf.at[i, x], x_buf.at[i, x], x_send.at[i, d - 1], x_recv.at[i, d - 1], x_peer(d))

    def send_x(i):
        for d in (1, 3, 2):
            b_copy(i, d).wait_recv()
        total = (b_buf[i, 0].astype(F32) + b_buf[i, 1].astype(F32)) + (
            b_buf[i, 2].astype(F32) + b_buf[i, 3].astype(F32))
        total = loads_v[i] * (1 - xh).astype(F32) - total
        x_buf[i, x] = total.astype(BF16)
        for d in (2, 1, 3):
            go(x_copy(i, d))

    def g_copy(i, d):
        mine = out_ref.at[i, :, cols(core, a)]
        return remote(own_u.at[i], mine, g_send.at[i, d - 1], g_recv.at[i, d - 1], a_peer(d))

    def p_copy(i, d):
        view = out_ref.at[i, :, cols(core, (a - d + 4) % 4)]
        source = own_u.at[i] if d == 0 else view
        return remote(source, view, p_send.at[i, d], p_recv.at[i, d], partner)

    def p_arrive(i, d):
        view = out_ref.at[i, :, cols(other, (b - d + 4) % 4)]
        return remote(view, view, p_send.at[i, d], p_recv.at[i, d], partner)

    def solve(i):
        for d in (1, 3, 2):
            x_copy(i, d).wait_recv()
        upper = x_buf[i, 0].astype(F32) + x_buf[i, 2].astype(F32)
        lower = x_buf[i, 1].astype(F32) + x_buf[i, 3].astype(F32)
        residual = jnp.concatenate([upper, lower], axis=0)
        if i > 0:
            residual = residual - coupled[...]
        residual = residual.astype(BF16)
        if i < steps - 1:
            u_all[pl.ds(i * block, block), :] = jnp.dot(
                inv_v[i].reshape(block, block), residual, preferred_element_type=F32).astype(BF16)
            mine = u_all[pl.ds(pl.multiple_of(i * block + xl * half, half), half), :]
        else:
            mine = jnp.dot(inv_v[i, xl], residual, preferred_element_type=F32).astype(BF16)
        own_u[i] = mine
        out_ref[i, :, cols(core, a)] = mine
        for d in (2, 1, 3):
            go(g_copy(i, d))
        go(p_copy(i, 0))
        if i < steps - 1:
            known = (i + 1) * block
            coupled[...] = jnp.dot(
                windows[i + 1][...].reshape(block, known), u_all[pl.ds(0, known), :],
                preferred_element_type=F32)

    def forward(i):
        for d in (1, 3, 2):
            view = out_ref.at[i, :, cols(core, (a - d + 4) % 4)]
            remote(own_u.at[i], view, g_send.at[i, d - 1], g_recv.at[i, d - 1], a_peer(d)).wait_recv()
            go(p_copy(i, d))

    for k in range(KPARTS):
        for copy in head[k]:
            copy.wait()
        if k + 3 < KPARTS:
            for copy in head[k + 3]:
                copy.start()
        elif k + 3 == KPARTS:
            own_half.start()
        elif k + 2 == KPARTS:
            panels[1].start()
        ks = pl.ds(k * kpart, kpart)
        part = jnp.dot(pv[0, :, ks], sv[0, ks, :], preferred_element_type=F32)
        acc[...] = part if k == 0 else acc[...] + part
        if k == 1:
            pl.semaphore_wait(barrier, len(greeted))
            for d in (0, 1):
                for copy in factor_send(d):
                    go(copy)
    send_core(0)
    for copy in panels[2:] + small:
        copy.start()

    def multiply(i, h):
        acc[...] = jnp.dot(pv[i], sv[h], preferred_element_type=F32)

    own_half.wait()
    multiply(0, 1)
    send_a(0)

    panels[1].wait()
    multiply(1, 0)
    send_core(1)
    multiply(1, 1)
    send_a(1)
    send_b(0)

    panels[2].wait()
    multiply(2, 0)
    send_core(2)
    multiply(2, 1)
    send_a(2)
    send_b(1)
    for copy in small:
        copy.wait()
    send_x(0)

    panels[3].wait()
    multiply(3, 0)
    send_core(3)
    forward_factor((0, 1))
    multiply(3, 1)
    send_a(3)
    send_b(2)
    forward_factor((2, 3))
    send_x(1)

    for d in (0, 1):
        for copy in factor_forwarded(d):
            copy.wait_recv()
    solve(0)
    send_b(3)
    send_x(2)
    solve(1)
    forward(0)
    send_x(3)
    solve(2)
    forward(1)
    solve(3)
    forward(2)
    forward(3)
    for i in range(steps):
        for d in range(4):
            p_arrive(i, d).wait_recv()
    for copy in started:
        copy.wait_send()


def shards(panel, solved, loads, window, inverses):
    steps, half, depth = panel.shape
    rhs = solved.shape[1]
    block = 2 * half
    width = rhs // 2
    vm = pltpu.VMEM
    dma = pltpu.SemaphoreType.DMA
    piece = (half, LANES)
    return pl.pallas_call(
        kernel,
        out_shape=pltpu.VMEM((steps, half, rhs), BF16),
        in_specs=[pl.BlockSpec(memory_space=pl.ANY)] * 5,
        out_specs=pl.BlockSpec(memory_space=pltpu.VMEM),
        scratch_shapes=[
            vm((steps, half, depth), BF16),
            vm((2, depth, width), BF16),
            vm((half, width), F32),
            vm((steps, half, width), BF16),
            vm((steps, half, width), BF16),
            vm((steps, 4) + piece, BF16),
            vm((steps, 3) + piece, BF16),
            vm((steps, 4) + piece, BF16),
            vm((steps, 4) + piece, BF16),
            vm((steps,) + piece, F32),
            vm((2, half, block), BF16),
            vm((2, half, 2 * block), BF16),
            vm((2, half, 3 * block), BF16),
            vm((steps, 2, half, block), BF16),
            vm(((steps - 1) * block, LANES), BF16),
            vm((block, LANES), F32),
            vm((steps,) + piece, BF16),
            dma((2 * KPARTS + 9,)),
            dma((2, 4)), dma((2, 4)), dma((2, 4)), dma((2, 4)),
            dma((steps,)), dma((steps,)),
            dma((steps, 3)), dma((steps, 3)),
            dma((steps, 3)), dma((steps, 3)),
            dma((steps, 3)), dma((steps, 3)),
            dma((steps, 3)), dma((steps, 3)),
            dma((steps, 4)), dma((steps, 4)),
        ],
        compiler_params=pltpu.CompilerParams(
            collective_id=0, has_side_effects=True, vmem_limit_bytes=56 * 2**20),
    )(panel, solved, loads, window, inverses)


def solution(mesh):
    placed = (
        P(None, "rows", "blk"),
        P("blk", None),
        P(None, "rows", None),
        P(None, "rows", None),
        P(None, "rows", None),
    )
    return jax.shard_map(
        shards, mesh=mesh, in_specs=placed, out_specs=P(None, "rows", None), check_vma=False
    )
```

time: 892 us -> 50.3 us (0.06)
  waiting for transfers between devices: 823 us -> 0 us
  Pallas kernels: 0 us -> 48.9 us
  matrix products: 41.4 us -> 0 us
  between operations: 13.6 us -> 0.01 us
    psum x1 -> x0, waiting for transfers between devices: 653 us -> none  [shards(): totals = lax.psum(partial_value, 'blk')]
    all_gather x7 -> x0, waiting for transfers between devices: 169 us -> none  [the longest x4 99.1 us: shards(): lax.all_gather(residual, 'rows', axis=0, tiled=True)]
    pallas_call x0 -> x1, Pallas kernels: none -> 48.9 us  [shards(): pl.pallas_call(kernel, out_shape=pltpu.VMEM((steps, half, rhs), BF16), in...]
    dot_general x11 -> x0, matrix products: 41.4 us -> none  [the longest x1 19 us: shards(): jnp.einsum('ksc,cr->ksr', panel, solved, preferred_element_type=jnp.float32)]
  transfers between devices with their start and end apart: 8 -> 0, of which waited for: 8 -> 0; matrix products, arithmetic and copies ran while one was open for 1% -> 0% of each run, Pallas kernels for 0% -> 0%
where the time goes in v1:
time: 50.3 us; the launch traced here: 50.2 us
  Pallas kernels  48.9 us (97%)
  local copies, waits for them, and re-layouts  1.32 us (3%)
    pallas_call x1, Pallas kernels, shards(): pl.pallas_call(kernel, out_shape=pltpu.VMEM((steps, half, rhs), BF16), in...  48.9 us
    unnamed x1, local copies, waits for them, and re-layouts  1.32 us

profile of v1, /device:TPU:1, one launch (start us, length us, event | category | flops | bytes accessed | tf_op | source)
XLA Modules:
  0.0 50.2 jit_solution(5126373677190622514)
XLA Ops:
  0.0 48.9 %shard_map.55 = bf16[4,256,1024]{2,1,0:T(8,128)(2,1)S(1)} custom-call(bf16[4,256,6144]{2,1,0:T(8,128)(2,1)} %panel_ref.1, bf16[6144,1024]{1,0:T(8,128)(2,1)} %solved_ref.1, f32[4,256,1024]{2,1,0:T(8,128)} %loads_ref.1, bf16[4,256,2048]{2,1,0:T(8,128)(2,1)} %window_ref.1, bf16[4,256,512]{2,1,0:T(8,128)(2,1)} %inv_ref.1), custom_call_target="tpu_custom_call" | custom-call | tf_op jit(solution)/shard_map/pallas_call | solution.py:321
  48.9 1.3 %copy.7 = bf16[4,256,1024]{2,1,0:T(8,128)(2,1)} copy(bf16[4,256,1024]{2,1,0:T(8,128)(2,1)S(1)} %shard_map.55) | data formatting | bytes 4194304
